TPU v7x, 32 devices: a whole 2x2x4 slice. The times are simulated.
32 devices in a mesh: leaf: 4 (over x, core), row: 4 (over z), col: 2 (over y).
Axes of the slice: x: 2, y: 2, z: 4, core: 2. Of those that a mesh axis runs over, the one named last changes fastest.
Arguments:
- widths: int32 [15], replicated, may hold values from 1024 to 2048, as said below
- bottom_lists: int32 [8, 32], P('leaf'), may hold values from 0 to 47, as said below
- root_inverse: bfloat16 [2048, 2048], P('row')
- second_panels: bfloat16 [4, 2048, 1024], P('leaf', 'row', 'col'), may hold values from -0.09375 to 0.09375
- second_inverse: bfloat16 [4, 1024, 2048], P('leaf', 'col', 'row')
- third_panels: bfloat16 [4, 2, 2048, 2048], P('leaf', None, 'row', 'col'), may hold values from -0.09375 to 0.09375
- third_inverse: bfloat16 [4, 2048, 2048], P('leaf', 'col', 'row')
- bottom_panels: bfloat16 [8, 4096, 2048], P('leaf', 'row', 'col'), may hold values from -0.09375 to 0.09375
- bottom_inverse: bfloat16 [8, 2048, 2048], P('leaf', 'col', 'row')
Outputs:
- second_off: bfloat16 [4, 2048, 1024], P('leaf', 'row', 'col')
- second_diag: bfloat16 [4, 1024, 2048], P('leaf', 'col', 'row')
- third_off: bfloat16 [4, 2, 2048, 2048], P('leaf', None, 'row', 'col')
- third_diag: bfloat16 [4, 2048, 2048], P('leaf', 'col', 'row')
- bottom_off: bfloat16 [8, 3, 2048, 2048], P('leaf', None, 'row', 'col')
- bottom_diag: bfloat16 [8, 2048, 2048], P('leaf', 'col', 'row')
Inputs may be any that keep to these rules, and one draw needn't show every extreme that they name: `widths`: some supernode has 2048 columns and some 2048/2. `bottom_lists`: row e lists 32 different blocks of 128 rows of its chain (root, then second-level ancestor, then parent, 16 blocks each) in increasing order; block 0 and all blocks of the parent are always listed.
All inputs are finite; a program needn't handle non-finite values.
Results may differ from a plain program's by a relative error of at most 0.015.
Values may be sent and summed in bfloat16 or wider, within the bound.
No kernel may reach another device: no remote copies, remote signals or barrier semaphores. Data moves between devices by JAX's collectives and lax.ppermute only.
A program may use at most 192 MiB of HBM per device.

v0:
```python
import jax
import jax.numpy as jnp
from jax import lax
from jax.sharding import PartitionSpec as P

NODES = 15
BOTTOM = 8


def partner(block, axis, apart):
    count = lax.axis_size(axis)
    route = []
    for low in range(count):
        high = low | 1 << apart
        if high != low and high < count:
            route += [(low, high), (high, low)]
    return lax.ppermute(block, axis, route)


def node_width(widths, node_at):
    return jnp.sum(jnp.where(jnp.arange(widths.shape[0]) == node_at, widths, 0))


def chain_fold(flat_chain, tile_width, ancestors, shard_piece):
    piece_rows = shard_piece.shape[1]
    picked = jnp.concatenate(
        [
            lax.dynamic_slice_in_dim(flat_chain, level_at * tile_width, piece_rows, 1)
            for level_at in range(ancestors)
        ],
        axis=1,
    )
    stacked = shard_piece.reshape(ancestors * piece_rows, shard_piece.shape[2])
    return jnp.dot(picked, stacked, preferred_element_type=jnp.float32)


def local(
    widths,
    bottom_lists,
    root_inverse,
    second_panels,
    second_inverse,
    third_panels,
    third_inverse,
    bottom_panels,
    bottom_inverse,
):
    group_at = lax.axis_index("leaf")
    row_at = lax.axis_index("row")
    col_at = lax.axis_index("col")
    rows_dev = root_inverse.shape[0]
    tile_width = root_inverse.shape[1]
    half_cols = second_panels.shape[2]
    own_cols = third_panels.shape[3]
    half_at = group_at % 2
    parent_one = 1 + group_at // 2
    node_two = 3 + group_at
    row_first = row_at * rows_dev
    row_index = row_first + jnp.arange(rows_dev)
    root_width = node_width(widths, 0)
    root_mask = (row_index < root_width)[:, None] & (jnp.arange(tile_width) < root_width)[None, :]
    root_block = jnp.where(root_mask, root_inverse, 0)
    width_one = node_width(widths, parent_one)
    mask_rows_one = row_index < width_one
    first_col = half_at * (tile_width // 2) + col_at * half_cols
    mask_cols_one = first_col + jnp.arange(half_cols) < width_one
    panel_one = jnp.where(mask_cols_one[None, :], second_panels[0], 0)
    shard_piece = lax.all_gather(panel_one, "row", axis=0, tiled=True)
    flat_piece = shard_piece
    product_one = jnp.dot(root_block, flat_piece, preferred_element_type=jnp.float32)
    off_one = (-product_one).astype(jnp.bfloat16)
    mine_half = lax.all_gather(off_one, "col", axis=1, tiled=True)
    other_half = partner(mine_half, "leaf", 0)
    off_full = jnp.where(
        half_at == 0,
        jnp.concatenate([mine_half, other_half], 1),
        jnp.concatenate([other_half, mine_half], 1),
    )
    term_one = lax.dot_general(
        panel_one, off_full, (((0,), (0,)), ((), ())), preferred_element_type=jnp.float32
    )
    summed_one = lax.psum_scatter(
        term_one.astype(jnp.bfloat16), "row", scatter_dimension=1, tiled=True
    ).astype(jnp.float32)
    inverse_one = jnp.where(
        mask_cols_one[:, None] & mask_rows_one[None, :], second_inverse[0], 0
    ).astype(jnp.float32)
    diag_one = (inverse_one - summed_one).astype(jnp.bfloat16)
    mine_diag = lax.all_gather(diag_one.T, "col", axis=1, tiled=True)
    other_diag = partner(mine_diag, "leaf", 0)
    diag_full = jnp.where(
        half_at == 0,
        jnp.concatenate([mine_diag, other_diag], 1),
        jnp.concatenate([other_diag, mine_diag], 1),
    )
    second_off = off_one[None]
    second_diag = diag_one[None]
    turned_one = lax.all_to_all(off_full, "row", split_axis=1, concat_axis=0, tiled=True)
    chain_two = jnp.stack(
        [jnp.concatenate([root_block, off_full], 1), jnp.concatenate([turned_one.T, diag_full], 1)],
        0,
    )
    flat_two = chain_two.reshape(2 * rows_dev, 2 * tile_width)
    first_own = col_at * own_cols
    width_two = node_width(widths, node_two)
    mask_cols_two = first_own + jnp.arange(own_cols) < width_two
    panel_two = jnp.where(mask_cols_two[None, None, :], third_panels[0], 0)
    product_two = chain_fold(
        flat_two, tile_width, 2, lax.all_gather(panel_two, "row", axis=1, tiled=True)
    )
    off_two = (-product_two).astype(jnp.bfloat16).reshape(2, rows_dev, own_cols)
    full_two = lax.all_gather(off_two, "col", axis=2, tiled=True)
    term_two = jnp.einsum("kin,kim->nm", panel_two, full_two, preferred_element_type=jnp.float32)
    summed_two = lax.psum_scatter(
        term_two.astype(jnp.bfloat16), "row", scatter_dimension=1, tiled=True
    ).astype(jnp.float32)
    mask_rows_two = row_index < width_two
    inverse_two = jnp.where(
        mask_cols_two[:, None] & mask_rows_two[None, :], third_inverse[0], 0
    ).astype(jnp.float32)
    diag_two = (inverse_two - summed_two).astype(jnp.bfloat16)
    diag_rows_two = lax.all_gather(diag_two.T, "col", axis=1, tiled=True)
    turned_two = lax.all_to_all(full_two, "row", split_axis=2, concat_axis=1, tiled=True)
    lower_two = jnp.transpose(turned_two, (2, 0, 1)).reshape(rows_dev, 2 * tile_width)
    chain_three = jnp.stack(
        [
            jnp.concatenate([chain_two[0], full_two[0]], 1),
            jnp.concatenate([chain_two[1], full_two[1]], 1),
            jnp.concatenate([lower_two, diag_rows_two], 1),
        ],
        0,
    )
    flat_three = chain_three.reshape(3 * rows_dev, 3 * tile_width)
    bottom_dev = bottom_panels.shape[0]
    list_len = bottom_lists.shape[1]
    block_rows = 2 * tile_width // list_len
    node_three = NODES - BOTTOM + bottom_dev * group_at + jnp.arange(bottom_dev)
    width_three = jnp.sum(
        jnp.where(jnp.arange(widths.shape[0])[None, :] == node_three[:, None], widths[None, :], 0),
        1,
    )
    mask_cols_three = (first_own + jnp.arange(own_cols))[None, :] < width_three[:, None]
    panel_three = jnp.where(mask_cols_three[:, None, :], bottom_panels, 0)
    positions = (
        jnp.repeat(bottom_lists, block_rows, axis=1) * block_rows
        + jnp.arange(list_len * block_rows) % block_rows
    )
    own_chain = (jnp.arange(3)[:, None] * tile_width + row_index[None, :]).reshape(-1)
    matches = bottom_lists[:, :, None] == (own_chain // block_rows)[None, None, :]
    member = jnp.any(matches, axis=1)
    slot_index = (
        jnp.sum(jnp.where(matches, jnp.arange(list_len)[None, :, None], 0), axis=1) * block_rows
        + own_chain % block_rows
    )
    shard_piece = lax.all_gather(panel_three, "row", axis=1, tiled=True)
    kept_rows = jnp.zeros((bottom_dev, 3 * rows_dev, own_cols), jnp.bfloat16)
    piece_rows = shard_piece.shape[1]
    columns = jnp.take(flat_three, positions.reshape(-1), axis=1).reshape(
        3 * rows_dev, bottom_dev, piece_rows
    )
    running = jnp.einsum("aec,ecn->ean", columns, shard_piece, preferred_element_type=jnp.float32)
    inside = member & (slot_index >= 0) & (slot_index < piece_rows)
    fetched = jax.vmap(lambda rows_in, picks: jnp.take(rows_in, picks, axis=0))(
        shard_piece, jnp.clip(slot_index, 0, piece_rows - 1)
    )
    kept_rows = jnp.where(inside[:, :, None], fetched, kept_rows)
    product_three, kept_rows = (running, kept_rows)
    chain_rows = kept_rows.reshape(bottom_dev, 3, rows_dev, own_cols)
    off_three = jnp.where(member[:, :, None], -product_three, 0.0).astype(jnp.bfloat16)
    off_three = off_three.reshape(bottom_dev, 3, rows_dev, own_cols)
    full_three = lax.all_gather(off_three, "col", axis=3, tiled=True)
    term_three = jnp.einsum(
        "ekin,ekim->enm", chain_rows, full_three, preferred_element_type=jnp.float32
    )
    summed_three = lax.psum_scatter(
        term_three.astype(jnp.bfloat16), "row", scatter_dimension=2, tiled=True
    ).astype(jnp.float32)
    mask_rows_three = row_index[None, :] < width_three[:, None]
    inverse_three = jnp.where(
        mask_cols_three[:, :, None] & mask_rows_three[:, None, :], bottom_inverse, 0
    ).astype(jnp.float32)
    diag_three = (inverse_three - summed_three).astype(jnp.bfloat16)
    return (second_off, second_diag, off_two[None], diag_two[None], off_three, diag_three)


def solution(mesh):
    in_specs = (
        P(),
        P("leaf", None),
        P("row", None),
        P("leaf", "row", "col"),
        P("leaf", "col", "row"),
        P("leaf", None, "row", "col"),
        P("leaf", "col", "row"),
        P("leaf", "row", "col"),
        P("leaf", "col", "row"),
    )
    out_specs = (
        P("leaf", "row", "col"),
        P("leaf", "col", "row"),
        P("leaf", None, "row", "col"),
        P("leaf", "col", "row"),
        P("leaf", None, "row", "col"),
        P("leaf", "col", "row"),
    )
    return jax.shard_map(local, mesh=mesh, in_specs=in_specs, out_specs=out_specs, check_vma=False)
```

profile of v0, /device:TPU:0, one launch (start us, length us, event | category | flops | bytes accessed | tf_op | source)
XLA Modules:
  0.0 1239.9 jit_solution(15678151634752697169)
XLA Ops:
  7.2 1.3 copy.59
  8.5 1.3 fusion.30
  9.8 0.7 add_compare_fusion
  10.5 0.9 bitcast_select_fusion.1
  11.5 0.7 fusion.26
  12.2 0.7 iota_compare_fusion
  12.8 2.3 and_select_fusion.1
  15.1 44.9 %all-gather.9.cloned.1.call-done = bf16[2048,512]{0,1:T(8,128)(2,1)} async-done(((bf16[512,512]{0,1:T(8,128)(2,1)}), bf16[2048,512]{0,1:T(8,128)(2,1)}) %all-gather.9.cloned.1.call-update) | async-done | bytes 2097168 | tf_op jit(solution)/shard_map/all_gather | solution.py:68
  60.0 3.7 fusion.12
  63.7 20.2 %all-gather.11.cloned.1.call-done = bf16[512,1024]{1,0:T(8,128)(2,1)} async-done(((bf16[512,512]{1,0:T(8,128)(2,1)}), bf16[512,1024]{1,0:T(8,128)(2,1)}) %all-gather.11.cloned.1.call-update) | async-done | bytes 1048592 | tf_op jit(solution)/shard_map/all_gather | solution.py:72
  83.9 2.9 collective-permute-done
  86.8 2.7 maximum_select_fusion
  89.5 1.3 copy-done
  90.8 2.6 convolution_convert_fusion
  93.6 2.0 copy.60
  95.6 0.7 fusion.25
  96.3 41.0 %reduce-scatter.4.cloned.1.call-done = bf16[512,512]{0,1:T(8,128)(2,1)} async-done(((bf16[512,2048]{0,1:T(8,128)(2,1)}), bf16[512,512]{0,1:T(8,128)(2,1)}) %reduce-scatter.4.cloned.1.call-update) | async-done | bytes 524304 | tf_op jit(solution)/shard_map/reduce_scatter | solution.py:82
  137.3 2.5 fusion.34
  140.4 3.0 bitcast_select_fusion
  143.6 1.3 copy.92
  144.9 1.6 maximum_select_fusion.1
  146.5 4.4 all-to-all-start
  151.0 9.4 all-gather.13.cloned.1.call-done
  160.4 3.9 maximum_bitcast_fusion.3
  164.4 75.8 %all-to-all-done = bf16[512,4,512]{2,0,1:T(8,128)(2,1)} async-done(((bf16[512,4,512]{2,0,1:T(8,128)(2,1)}), bf16[512,4,512]{2,0,1:T(8,128)(2,1)}, u32[]{:S(2)}, u32[]{:S(2)}) %all-to-all-start) | async-done | bytes 2097184 | tf_op jit(solution)/shard_map/all_to_all | solution.py:98
  240.1 3.9 copy.81
  244.1 2.5 maximum_select_fusion.2
  246.6 1.4 copy-done.4
  248.0 2.5 maximum_bitcast_fusion.4
  250.5 7.5 pad_maximum_fusion.1
  258.0 76.6 %all-gather.15.cloned.1.call-done = bf16[2,2048,1024]{2,1,0:T(8,128)(2,1)} async-done(((bf16[2,512,1024]{2,1,0:T(8,128)(2,1)}), bf16[2,2048,1024]{2,1,0:T(8,128)(2,1)}) %all-gather.15.cloned.1.call-update) | async-done | bytes 8388624 | tf_op jit(solution)/shard_map/all_gather | solution.py:109
  334.5 14.6 %negate_convert_fusion = bf16[1024,1024]{1,0:T(8,128)(2,1)} fusion(bf16[1024,4096]{1,0:T(8,128)(2,1)} %bitcast.115, bf16[4096,1024]{1,0:T(8,128)(2,1)} %bitcast.128), kind=kOutput, calls=%fused_computation.21 | convolution fusion | flops 8592031744 | bytes 18874368 | tf_op jit(solution)/shard_map/dot_general | solution.py:34
  349.2 12.2 reduce-scatter.6.cloned.1.call-start
  361.4 43.7 %all-gather.17.cloned.1.call-done = bf16[2,512,2048]{2,1,0:T(8,128)(2,1)} async-done(((bf16[2,512,1024]{2,1,0:T(8,128)(2,1)}), bf16[2,512,2048]{2,1,0:T(8,128)(2,1)}) %all-gather.17.cloned.1.call-update) | async-done | bytes 4194320 | tf_op jit(solution)/shard_map/all_gather | solution.py:112
  405.1 9.4 bitcast_convert_fusion.1
  414.6 1.5 copy.67
  416.6 74.8 %reduce-scatter.6.cloned.1.call-done = bf16[1024,512]{0,1:T(8,128)(2,1)} async-done(((bf16[1024,2048]{0,1:T(8,128)(2,1)}), bf16[1024,512]{0,1:T(8,128)(2,1)}) %reduce-scatter.6.cloned.1.call-update) | async-done | bytes 1048592 | tf_op jit(solution)/shard_map/reduce_scatter | solution.py:114
  491.5 3.1 fusion.36
  496.0 4.4 broadcast_select_fusion
  500.5 11.2 copy.70
  511.8 5.0 all-to-all-start.1
  516.9 0.7 add_select_fusion.2
  519.0 2.9 slice_bitcast_fusion.1
  522.5 0.6 copy-done.5
  523.1 5.1 maximum_bitcast_fusion
  528.2 191.2 %all-to-all-done.1 = bf16[2,512,2048]{1,0,2:T(2,128)(2,1)} async-done(((bf16[2,512,2048]{1,0,2:T(2,128)(2,1)}), bf16[2,512,2048]{1,0,2:T(2,128)(2,1)}, u32[]{:S(2)}, u32[]{:S(2)}) %all-to-all-start.1) | async-done | bytes 4194336 | tf_op jit(solution)/shard_map/all_to_all | solution.py:123
  719.4 5.1 copy.85
  724.5 4.5 copy.87
  728.9 6.4 maximum_bitcast_fusion.2
  735.4 12.1 pad_maximum_fusion
  747.5 24.7 %copy.72 = bf16[1536,6144]{0,1:T(8,128)(2,1)} copy(bf16[1536,6144]{1,0:T(8,128)(2,1)} %bitcast.107) | data formatting | bytes 37748736 | tf_op jit(solution)/shard_map/reshape | solution.py:133
  772.2 58.3 %gather_fusion = bf16[8192,1536]{1,0:T(8,128)(2,1)} fusion(bf16[1536,6144]{0,1:T(8,128)(2,1)} %copy.72, s32[8192]{0:T(1024)S(1)} %broadcast_clamp_fusion), kind=kCustom, calls=%fused_computation | custom fusion | bytes 50364416 | tf_op jit(solution)/shard_map/jit(_take)/gather | solution.py:158
  830.5 32.1 %copy.73 = bf16[1536,2,4096]{2,0,1:T(8,128)(2,1)} copy(bf16[1536,2,4096]{0,2,1:T(8,128)(2,1)} %bitcast.106) | data formatting | bytes 50331648 | tf_op jit(solution)/shard_map/jit(_take)/gather | solution.py:158
  862.5 18.1 %all-gather.21.cloned.1.call-done = bf16[2,4096,1024]{2,1,0:T(8,128)(2,1)} async-done(((bf16[2,1024,1024]{2,1,0:T(8,128)(2,1)}), bf16[2,4096,1024]{2,1,0:T(8,128)(2,1)}) %all-gather.21.cloned.1.call-update) | async-done | bytes 16777232 | tf_op jit(solution)/shard_map/all_gather | solution.py:155
  880.7 33.0 %select_convert_fusion = bf16[2,1536,1024]{2,1,0:T(8,128)(2,1)} fusion(bf16[2,4096,1024]{2,1,0:T(8,128)(2,1)} %all-gather.21.cloned.1.call-done, bf16[1536,2,4096]{2,0,1:T(8,128)(2,1)} %copy.73, pred[2,4096]{1,0:T(4,128)(4,1)S(1)} %compare_and_fusion, pred[2,1536]{1,0:T(4,128)(4,1)S(1)} %compare_reduce_fusion), kind=kOutput, calls=%fused_computation.7 | convolution fusion | flops 25791823872 | bytes 48245760 | tf_op jit(solution)/shard_map/aec,ecn->ean/dot_general | solution.py:161
  914.7 62.6 %gather_fusion.1 = bf16[3072,1024]{1,0:T(8,128)(2,1)} fusion(bf16[2,4096,1024]{2,1,0:T(8,128)(2,1)} %all-gather.21.cloned.1.call-done, s32[3072]{0:T(1024)S(1)} %reshape.373), kind=kCustom, calls=%fused_computation.1 | custom fusion | bytes 12607488 | tf_op jit(solution)/shard_map/vmap(jit(_take))/gather | solution.py:163
  977.3 8.7 copy.74
  986.0 79.0 %all-gather.23.cloned.1.call-done = bf16[2,3,512,2048]{3,2,1,0:T(8,128)(2,1)} async-done(((bf16[2,3,512,1024]{3,2,1,0:T(8,128)(2,1)}), bf16[2,3,512,2048]{3,2,1,0:T(8,128)(2,1)}) %all-gather.23.cloned.1.call-update) | async-done | bytes 12582928 | tf_op jit(solution)/shard_map/all_gather | solution.py:171
  1064.9 20.0 %bitcast_convert_fusion = bf16[2,1024,2048]{2,1,0:T(8,128)(2,1)} fusion(bf16[2,3,512,2048]{3,2,1,0:T(8,128)(2,1)} %all-gather.23.cloned.1.call-done, bf16[2,3,512,1024]{2,3,1,0:T(8,128)(2,1)} %copy.74, pred[2,3,512]{2,1,0:T(4,128)(4,1)S(1)} %get-tuple-element.40, pred[2,3,512]{2,1,0:T(4,128)(4,1)S(1)} %get-tuple-element.39), kind=kOutput, calls=%fused_computation.6 | convolution fusion | flops 12895387648 | bytes 27269120 | tf_op jit(solution)/shard_map/ekin,ekim->enm/dot_general | solution.py:172
  1084.9 0.6 copy-done.19
  1085.6 2.3 copy.75
  1087.9 1.3 copy.76
  1089.2 140.5 %reduce-scatter.8.cloned.1.call-done = bf16[2,1024,512]{2,1,0:T(8,128)(2,1)} async-done(((bf16[2,1024,2048]{2,1,0:T(8,128)(2,1)}), bf16[2,1024,512]{2,1,0:T(8,128)(2,1)}) %reduce-scatter.8.cloned.1.call-update) | async-done | bytes 2097168 | tf_op jit(solution)/shard_map/reduce_scatter | solution.py:175
  1229.7 3.2 subtract_convert_fusion
  (105 shorter events, 6.2 us)
Async XLA Ops:
  7.2 52.8 %all-gather.9.cloned.1.call-start = ((), (), s32[]{:S(2)}) async-start(), calls=%async_computation.5 | async-start | bytes 2621440 | tf_op jit(solution)/shard_map/all_gather | solution.py:68
  11.4 72.5 %all-gather.11.cloned.1.call-start = ((), (), s32[]{:S(2)}) async-start(), calls=%async_computation.6 | async-start | bytes 1572864 | tf_op jit(solution)/shard_map/all_gather | solution.py:72
  63.7 73.6 %reduce-scatter.4.cloned.1.call-start = ((), (), s32[]{:S(2)}) async-start(), calls=%async_computation.7 | async-start | bytes 2621440 | tf_op jit(solution)/shard_map/reduce_scatter | solution.py:82
  83.9 2.9 collective-permute-start
  83.9 6.9 copy-start.10
  86.8 6.7 copy-start.8
  89.5 1.4 copy-start
  93.5 66.9 %all-gather.13.cloned.1.call-start = ((), (), s32[]{:S(2)}) async-start(), calls=%async_computation.8 | async-start | bytes 1572864 | tf_op jit(solution)/shard_map/all_gather | solution.py:89
  96.3 47.2 %copy-start.7 = (bf16[512,1024]{1,0:T(8,128)(2,1)S(1)}, bf16[512,1024]{1,0:T(8,128)(2,1)}, u32[]{:S(2)}) copy-start(bf16[512,1024]{1,0:T(8,128)(2,1)} %all-gather.11.cloned.1.call-done) | copy-start | bytes 3145732
  139.8 194.7 %all-gather.15.cloned.1.call-start = ((), (), s32[]{:S(2)}) async-start(), calls=%async_computation.9 | async-start | bytes 10485760 | tf_op jit(solution)/shard_map/all_gather | solution.py:109
  146.5 93.6 %all-to-all-start = ((bf16[512,4,512]{2,0,1:T(8,128)(2,1)}), bf16[512,4,512]{2,0,1:T(8,128)(2,1)}, u32[]{:S(2)}, u32[]{:S(2)}) async-start(bf16[512,4,512]{2,0,1:T(8,128)(2,1)} %maximum_select_fusion.1), calls=%async_computation.1 | async-start | bytes 4194304 | tf_op jit(solution)/shard_map/all_to_all | solution.py:98
  151.0 254.1 %all-gather.17.cloned.1.call-start = ((), (), s32[]{:S(2)}) async-start(), calls=%async_computation.10 | async-start | bytes 6291456 | tf_op jit(solution)/shard_map/all_gather | solution.py:112
  160.4 83.6 %collective-permute-start.1 = (bf16[512,1024]{1,0:T(8,128)(2,1)}, bf16[512,1024]{1,0:T(8,128)(2,1)}, u32[]{:S(2)}, u32[]{:S(2)}) collective-permute-start(bf16[512,1024]{1,0:T(8,128)(2,1)} %all-gather.13.cloned.1.call-done), channel_id=1, source_target_pairs={{0,8},{8,0},{16,24},{24,16},{1,9},{9,1},{17,25},{25,17},{2,10},{10... | collective-permute-start | bytes 3145736 | tf_op jit(solution)/shard_map/ppermute | solution.py:17
  164.4 79.7 %copy-start.11 = (bf16[512,1024]{1,0:T(8,128)(2,1)S(1)}, bf16[512,1024]{1,0:T(8,128)(2,1)}, u32[]{:S(2)}) copy-start(bf16[512,1024]{1,0:T(8,128)(2,1)} %all-gather.13.cloned.1.call-done) | copy-start | bytes 3145732
  244.0 3.9 copy-start.2
  246.6 1.4 copy-start.4
  349.2 142.3 %reduce-scatter.6.cloned.1.call-start = ((), (), s32[]{:S(2)}) async-start(), calls=%async_computation.11 | async-start | bytes 5242880 | tf_op jit(solution)/shard_map/reduce_scatter | solution.py:114
  414.5 80.1 %copy-start.24 = (s32[15]{0:T(128)S(1)}, s32[15]{0:T(128)}, u32[]{:S(2)}) copy-start(s32[15]{0:T(128)} %param.9) | copy-start | bytes 184
  414.5 314.4 %all-gather.19.cloned.1.call-start = ((), (), s32[]{:S(2)}) async-start(), calls=%async_computation.12 | async-start | bytes 3145728 | tf_op jit(solution)/shard_map/all_gather | solution.py:122
  494.6 386.1 %all-gather.21.cloned.1.call-start = ((), (), s32[]{:S(2)}) async-start(), calls=%async_computation.13 | async-start | bytes 20971520 | tf_op jit(solution)/shard_map/all_gather | solution.py:155
  494.8 0.5 copy-start.22
  495.5 0.6 copy-start.14
  511.8 6.4 copy-start.20
  511.8 207.6 %all-to-all-start.1 = ((bf16[2,512,2048]{1,0,2:T(2,128)(2,1)}), bf16[2,512,2048]{1,0,2:T(2,128)(2,1)}, u32[]{:S(2)}, u32[]{:S(2)}) async-start(bf16[2,512,2048]{1,0,2:T(2,128)(2,1)} %copy.70), calls=%async_computation.3 | async-start | bytes 8388608 | tf_op jit(solution)/shard_map/all_to_all | solution.py:123
  516.8 548.2 %all-gather.23.cloned.1.call-start = ((), (), s32[]{:S(2)}) async-start(), calls=%async_computation.14 | async-start | bytes 18874368 | tf_op jit(solution)/shard_map/all_gather | solution.py:171
  516.9 0.7 copy-start.18
  518.2 0.6 copy-start.12
  519.0 2.9 copy-start.1
  519.0 3.5 copy-start.3
  519.0 4.1 copy-start.5
  728.9 6.4 slice-start
  728.9 6.4 slice-start.1
  913.6 0.7 copy-start.13
  913.7 0.7 copy-start.21
  913.7 0.8 copy-start.17
  913.7 0.9 copy-start.16
  913.7 316.0 %reduce-scatter.8.cloned.1.call-start = ((), (), s32[]{:S(2)}) async-start(), calls=%async_computation.15 | async-start | bytes 10485760 | tf_op jit(solution)/shard_map/reduce_scatter | solution.py:175
  1084.9 0.7 copy-start.19
  1084.9 0.7 copy-start.23
  1084.9 3.0 copy-start.6
  1084.9 144.8 %copy-start.9 = (bf16[2,1024,512]{2,1,0:T(8,128)(2,1)S(1)}, bf16[2,1024,512]{2,1,0:T(8,128)(2,1)}, u32[]{:S(2)}) copy-start(bf16[2,1024,512]{2,1,0:T(8,128)(2,1)} %param.17) | copy-start | bytes 6291460
  1084.9 144.8 %copy-start.15 = (pred[2,1024]{1,0:T(4,128)(4,1)S(1)}, pred[2,1024]{1,0:T(4,128)(4,1)}, u32[]{:S(2)}) copy-start(pred[2,1024]{1,0:T(4,128)(4,1)} %copy-done.14) | copy-start | bytes 6148
Sparse Core Ops, SparseCore 0:
  11.6 48.3 all-gather.8
  63.8 20.0 all-gather.10
  93.6 43.6 reduce-scatter.3
  139.9 20.4 all-gather.12
  161.9 172.6 all-gather.14
  349.3 55.7 all-gather.16
  414.6 76.7 reduce-scatter.5
  494.7 33.6 all-gather.18
  529.9 350.6 all-gather.20
  913.8 151.0 all-gather.22
  1085.1 144.6 reduce-scatter.7
where the time goes:
time: 1250 us; the launch traced here: 1240 us
  waiting for transfers between devices  818 us (65%)
  local copies, waits for them, and re-layouts  231 us (18%)
  matrix products  83.3 us (7%)
  other arithmetic  71.1 us (6%)
  starting transfers between devices  22 us (2%)
  between operations  14.7 us (1%)
    all_to_all x1, waiting for transfers between devices, local(): lax.all_to_all(full_two, 'row', split_axis=2, concat_axis=1, tiled=True)  191 us
    reduce_scatter x1, waiting for transfers between devices, local(): lax.psum_scatter(term_three.astype(jnp.bfloat16), 'row', scatter_dimensio...  141 us
    gather x2, local copies, waits for them, and re-layouts, local(): jnp.take(flat_three, positions.reshape(-1), axis=1)  90.3 us
    all_gather x1, waiting for transfers between devices, local(): full_three = lax.all_gather(off_three, 'col', axis=3, tiled=True)  79 us
    all_gather x1, waiting for transfers between devices, local(): lax.all_gather(panel_two, 'row', axis=1, tiled=True)  76.6 us
    all_to_all x1, waiting for transfers between devices, local(): lax.all_to_all(off_full, 'row', split_axis=1, concat_axis=0, tiled=True)  75.8 us
    reduce_scatter x1, waiting for transfers between devices, local(): lax.psum_scatter(term_two.astype(jnp.bfloat16), 'row', scatter_dimension=...  74.8 us
    gather x3, local copies, waits for them, and re-layouts, local(): jnp.take(rows_in, picks, axis=0)  71.3 us
  transfers between devices with their start and end apart: 15, of which 13 were waited for; matrix products, arithmetic and copies ran while one was open for 23% of the time, Pallas kernels for 0%

commit v1 on v0

--- a/solution.py
+++ b/solution.py
@@ -95,7 +95,10 @@
     )
     second_off = off_one[None]
     second_diag = diag_one[None]
-    turned_one = lax.all_to_all(off_full, "row", split_axis=1, concat_axis=0, tiled=True)
+    turned_one = jnp.concatenate(
+        lax.all_to_all(jnp.stack(jnp.split(off_full, lax.axis_size("row"), axis=1)), "row", 0, 0),
+        axis=0,
+    )
     chain_two = jnp.stack(
         [jnp.concatenate([root_block, off_full], 1), jnp.concatenate([turned_one.T, diag_full], 1)],
         0,

time: 1250 us -> 1250 us (level)
  transfers between devices with their start and end apart: 15 -> 15, of which waited for: 13 -> 13; matrix products, arithmetic and copies ran while one was open for 23% -> 22% of each run, Pallas kernels for 0% -> 0%
where the time goes in v1:
time: 1250 us; the launch traced here: 1240 us
  waiting for transfers between devices  820 us (66%)
  local copies, waits for them, and re-layouts  226 us (18%)
  matrix products  83.2 us (7%)
  other arithmetic  71.5 us (6%)
  starting transfers between devices  22 us (2%)
  between operations  14.7 us (1%)
    all_to_all x1, waiting for transfers between devices, local(): lax.all_to_all(full_two, 'row', split_axis=2, concat_axis=1, tiled=True)  191 us
    reduce_scatter x1, waiting for transfers between devices, local(): lax.psum_scatter(term_three.astype(jnp.bfloat16), 'row', scatter_dimensio...  141 us
    gather x2, local copies, waits for them, and re-layouts, local(): jnp.take(flat_three, positions.reshape(-1), axis=1)  90.3 us
    all_gather x1, waiting for transfers between devices, local(): lax.all_gather(panel_two, 'row', axis=1, tiled=True)  82.6 us
    all_gather x1, waiting for transfers between devices, local(): full_three = lax.all_gather(off_three, 'col', axis=3, tiled=True)  79 us
    reduce_scatter x1, waiting for transfers between devices, local(): lax.psum_scatter(term_two.astype(jnp.bfloat16), 'row', scatter_dimension=...  74.7 us
    gather x3, local copies, waits for them, and re-layouts, local(): jnp.take(rows_in, picks, axis=0)  71.3 us
    all_to_all x1, waiting for transfers between devices, local(): lax.all_to_all(jnp.stack(jnp.split(off_full, lax.axis_size('row'), axis=1...  68.4 us
  transfers between devices with their start and end apart: 15, of which 13 were waited for; matrix products, arithmetic and copies ran while one was open for 22% of the time, Pallas kernels for 0%

profile of v1, /device:TPU:0, one launch (start us, length us, event | category | flops | bytes accessed | tf_op | source)
XLA Modules:
  0.0 1237.6 jit_solution(8056756718153811453)
XLA Ops:
  7.2 1.3 copy.55
  8.5 1.3 fusion.30
  9.8 0.7 add_compare_fusion
  10.5 0.9 bitcast_select_fusion.1
  11.5 0.7 fusion.26
  12.2 0.7 iota_compare_fusion
  12.8 2.3 and_select_fusion.1
  15.1 44.9 %all-gather.9.cloned.1.call-done = bf16[2048,512]{0,1:T(8,128)(2,1)} async-done(((bf16[512,512]{0,1:T(8,128)(2,1)}), bf16[2048,512]{0,1:T(8,128)(2,1)}) %all-gather.9.cloned.1.call-update) | async-done | bytes 2097168 | tf_op jit(solution)/shard_map/all_gather | solution.py:68
  60.0 3.7 fusion.12
  63.7 20.2 %all-gather.11.cloned.1.call-done = bf16[512,1024]{1,0:T(8,128)(2,1)} async-done(((bf16[512,512]{1,0:T(8,128)(2,1)}), bf16[512,1024]{1,0:T(8,128)(2,1)}) %all-gather.11.cloned.1.call-update) | async-done | bytes 1048592 | tf_op jit(solution)/shard_map/all_gather | solution.py:72
  83.9 3.0 collective-permute-done
  86.9 3.0 maximum_select_fusion
  90.0 2.6 convolution_convert_fusion
  92.9 0.7 fusion.25
  93.5 42.9 %reduce-scatter.4.cloned.1.call-done = bf16[512,512]{0,1:T(8,128)(2,1)} async-done(((bf16[512,2048]{0,1:T(8,128)(2,1)}), bf16[512,512]{0,1:T(8,128)(2,1)}) %reduce-scatter.4.cloned.1.call-update) | async-done | bytes 524304 | tf_op jit(solution)/shard_map/reduce_scatter | solution.py:82
  136.4 2.3 fusion.34
  138.8 0.7 broadcast_compare_fusion.2
  139.4 3.0 bitcast_select_fusion
  142.7 1.6 pad_maximum_fusion.2
  144.3 4.4 all-to-all-start
  148.8 10.6 all-gather.13.cloned.1.call-done
  159.4 3.9 maximum_bitcast_fusion.3
  163.3 68.4 %all-to-all-done = bf16[4,512,512]{2,1,0:T(8,128)(2,1)} async-done(((bf16[4,512,512]{2,1,0:T(8,128)(2,1)}), bf16[4,512,512]{2,1,0:T(8,128)(2,1)}, u32[]{:S(2)}, u32[]{:S(2)}) %all-to-all-start) | async-done | bytes 2097184 | tf_op jit(solution)/shard_map/all_to_all | solution.py:99
  231.8 3.9 copy.73
  235.7 2.5 maximum_select_fusion.1
  238.2 1.4 copy-done.4
  239.6 2.5 maximum_bitcast_fusion.4
  242.1 7.6 pad_maximum_fusion.1
  249.7 82.6 %all-gather.15.cloned.1.call-done = bf16[2,2048,1024]{2,1,0:T(8,128)(2,1)} async-done(((bf16[2,512,1024]{2,1,0:T(8,128)(2,1)}), bf16[2,2048,1024]{2,1,0:T(8,128)(2,1)}) %all-gather.15.cloned.1.call-update) | async-done | bytes 8388624 | tf_op jit(solution)/shard_map/all_gather | solution.py:112
  332.3 14.6 %negate_convert_fusion = bf16[1024,1024]{1,0:T(8,128)(2,1)} fusion(bf16[1024,4096]{1,0:T(8,128)(2,1)} %bitcast.113, bf16[4096,1024]{1,0:T(8,128)(2,1)} %bitcast.122), kind=kOutput, calls=%fused_computation.21 | convolution fusion | flops 8592031744 | bytes 18874368 | tf_op jit(solution)/shard_map/dot_general | solution.py:34
  347.0 12.2 reduce-scatter.6.cloned.1.call-start
  359.2 43.7 %all-gather.17.cloned.1.call-done = bf16[2,512,2048]{2,1,0:T(8,128)(2,1)} async-done(((bf16[2,512,1024]{2,1,0:T(8,128)(2,1)}), bf16[2,512,2048]{2,1,0:T(8,128)(2,1)}) %all-gather.17.cloned.1.call-update) | async-done | bytes 4194320 | tf_op jit(solution)/shard_map/all_gather | solution.py:115
  402.9 9.4 bitcast_convert_fusion.1
  412.3 1.5 copy.59
  413.8 0.7 fusion.24
  414.5 74.7 %reduce-scatter.6.cloned.1.call-done = bf16[1024,512]{0,1:T(8,128)(2,1)} async-done(((bf16[1024,2048]{0,1:T(8,128)(2,1)}), bf16[1024,512]{0,1:T(8,128)(2,1)}) %reduce-scatter.6.cloned.1.call-update) | async-done | bytes 1048592 | tf_op jit(solution)/shard_map/reduce_scatter | solution.py:117
  489.2 3.1 fusion.36
  493.8 4.4 broadcast_select_fusion
  498.3 11.2 copy.62
  509.5 5.0 all-to-all-start.1
  514.7 0.7 add_select_fusion.2
  515.3 0.6 add_select_fusion.1
  516.8 2.9 slice_bitcast_fusion.1
  520.2 0.6 copy-done.5
  520.9 5.1 maximum_bitcast_fusion
  526.0 191.2 %all-to-all-done.1 = bf16[2,512,2048]{1,0,2:T(2,128)(2,1)} async-done(((bf16[2,512,2048]{1,0,2:T(2,128)(2,1)}), bf16[2,512,2048]{1,0,2:T(2,128)(2,1)}, u32[]{:S(2)}, u32[]{:S(2)}) %all-to-all-start.1) | async-done | bytes 4194336 | tf_op jit(solution)/shard_map/all_to_all | solution.py:126
  717.2 5.1 copy.75
  722.2 4.5 copy.77
  726.7 6.4 maximum_bitcast_fusion.2
  733.1 12.1 pad_maximum_fusion
  745.2 24.7 %copy.64 = bf16[1536,6144]{0,1:T(8,128)(2,1)} copy(bf16[1536,6144]{1,0:T(8,128)(2,1)} %bitcast.105) | data formatting | bytes 37748736 | tf_op jit(solution)/shard_map/reshape | solution.py:136
  770.0 58.3 %gather_fusion = bf16[8192,1536]{1,0:T(8,128)(2,1)} fusion(bf16[1536,6144]{0,1:T(8,128)(2,1)} %copy.64, s32[8192]{0:T(1024)S(1)} %broadcast_clamp_fusion), kind=kCustom, calls=%fused_computation | custom fusion | bytes 50364416 | tf_op jit(solution)/shard_map/jit(_take)/gather | solution.py:161
  828.2 32.1 %copy.65 = bf16[1536,2,4096]{2,0,1:T(8,128)(2,1)} copy(bf16[1536,2,4096]{0,2,1:T(8,128)(2,1)} %bitcast.104) | data formatting | bytes 50331648 | tf_op jit(solution)/shard_map/jit(_take)/gather | solution.py:161
  860.3 18.1 %all-gather.21.cloned.1.call-done = bf16[2,4096,1024]{2,1,0:T(8,128)(2,1)} async-done(((bf16[2,1024,1024]{2,1,0:T(8,128)(2,1)}), bf16[2,4096,1024]{2,1,0:T(8,128)(2,1)}) %all-gather.21.cloned.1.call-update) | async-done | bytes 16777232 | tf_op jit(solution)/shard_map/all_gather | solution.py:158
  878.4 33.0 %select_convert_fusion = bf16[2,1536,1024]{2,1,0:T(8,128)(2,1)} fusion(bf16[2,4096,1024]{2,1,0:T(8,128)(2,1)} %all-gather.21.cloned.1.call-done, bf16[1536,2,4096]{2,0,1:T(8,128)(2,1)} %copy.65, pred[2,4096]{1,0:T(4,128)(4,1)S(1)} %compare_and_fusion, pred[2,1536]{1,0:T(4,128)(4,1)S(1)} %compare_reduce_fusion), kind=kOutput, calls=%fused_computation.7 | convolution fusion | flops 25791823872 | bytes 48245760 | tf_op jit(solution)/shard_map/aec,ecn->ean/dot_general | solution.py:164
  912.4 62.6 %gather_fusion.1 = bf16[3072,1024]{1,0:T(8,128)(2,1)} fusion(bf16[2,4096,1024]{2,1,0:T(8,128)(2,1)} %all-gather.21.cloned.1.call-done, s32[3072]{0:T(1024)S(1)} %reshape.370), kind=kCustom, calls=%fused_computation.1 | custom fusion | bytes 12607488 | tf_op jit(solution)/shard_map/vmap(jit(_take))/gather | solution.py:166
  975.1 8.7 copy.66
  983.7 79.0 %all-gather.23.cloned.1.call-done = bf16[2,3,512,2048]{3,2,1,0:T(8,128)(2,1)} async-done(((bf16[2,3,512,1024]{3,2,1,0:T(8,128)(2,1)}), bf16[2,3,512,2048]{3,2,1,0:T(8,128)(2,1)}) %all-gather.23.cloned.1.call-update) | async-done | bytes 12582928 | tf_op jit(solution)/shard_map/all_gather | solution.py:174
  1062.7 20.0 %bitcast_convert_fusion = bf16[2,1024,2048]{2,1,0:T(8,128)(2,1)} fusion(bf16[2,3,512,2048]{3,2,1,0:T(8,128)(2,1)} %all-gather.23.cloned.1.call-done, bf16[2,3,512,1024]{2,3,1,0:T(8,128)(2,1)} %copy.66, pred[2,3,512]{2,1,0:T(4,128)(4,1)S(1)} %get-tuple-element.44, pred[2,3,512]{2,1,0:T(4,128)(4,1)S(1)} %get-tuple-element.43), kind=kOutput, calls=%fused_computation.6 | convolution fusion | flops 12895387648 | bytes 27269120 | tf_op jit(solution)/shard_map/ekin,ekim->enm/dot_general | solution.py:175
  1082.7 0.6 copy-done.18
  1083.4 2.3 copy.67
  1085.7 1.3 copy.68
  1087.0 140.5 %reduce-scatter.8.cloned.1.call-done = bf16[2,1024,512]{2,1,0:T(8,128)(2,1)} async-done(((bf16[2,1024,2048]{2,1,0:T(8,128)(2,1)}), bf16[2,1024,512]{2,1,0:T(8,128)(2,1)}) %reduce-scatter.8.cloned.1.call-update) | async-done | bytes 2097168 | tf_op jit(solution)/shard_map/reduce_scatter | solution.py:178
  1227.5 3.2 subtract_convert_fusion
  (102 shorter events, 4.8 us)
Async XLA Ops:
  7.2 52.8 %all-gather.9.cloned.1.call-start = ((), (), s32[]{:S(2)}) async-start(), calls=%async_computation.5 | async-start | bytes 2621440 | tf_op jit(solution)/shard_map/all_gather | solution.py:68
  11.4 72.5 %all-gather.11.cloned.1.call-start = ((), (), s32[]{:S(2)}) async-start(), calls=%async_computation.6 | async-start | bytes 1572864 | tf_op jit(solution)/shard_map/all_gather | solution.py:72
  15.1 48.6 %copy-start = (bf16[512,2048]{1,0:T(8,128)(2,1)}, bf16[512,2048]{1,0:T(8,128)(2,1)S(1)}, u32[]{:S(2)}) copy-start(bf16[512,2048]{1,0:T(8,128)(2,1)S(1)} %and_select_fusion.1) | copy-start | bytes 6291460
  63.7 26.3 %copy-start.8 = (bf16[512,512]{0,1:T(8,128)(2,1)S(1)}, bf16[512,512]{0,1:T(8,128)(2,1)}, u32[]{:S(2)}) copy-start(bf16[512,512]{0,1:T(8,128)(2,1)} %bitcast_select_fusion.1) | copy-start | bytes 1572868
  63.7 72.7 %reduce-scatter.4.cloned.1.call-start = ((), (), s32[]{:S(2)}) async-start(), calls=%async_computation.7 | async-start | bytes 2621440 | tf_op jit(solution)/shard_map/reduce_scatter | solution.py:82
  83.9 3.0 collective-permute-start
  89.9 2.7 copy-start.10
  92.6 66.8 %all-gather.13.cloned.1.call-start = ((), (), s32[]{:S(2)}) async-start(), calls=%async_computation.8 | async-start | bytes 1572864 | tf_op jit(solution)/shard_map/all_gather | solution.py:89
  138.7 193.6 %all-gather.15.cloned.1.call-start = ((), (), s32[]{:S(2)}) async-start(), calls=%async_computation.9 | async-start | bytes 10485760 | tf_op jit(solution)/shard_map/all_gather | solution.py:112
  144.3 87.4 %all-to-all-start = ((bf16[4,512,512]{2,1,0:T(8,128)(2,1)}), bf16[4,512,512]{2,1,0:T(8,128)(2,1)}, u32[]{:S(2)}, u32[]{:S(2)}) async-start(bf16[4,512,512]{2,1,0:T(8,128)(2,1)} %pad_maximum_fusion.2), calls=%async_computation.1 | async-start | bytes 4194304 | tf_op jit(solution)/shard_map/all_to_all | solution.py:99
  148.8 254.1 %all-gather.17.cloned.1.call-start = ((), (), s32[]{:S(2)}) async-start(), calls=%async_computation.10 | async-start | bytes 6291456 | tf_op jit(solution)/shard_map/all_gather | solution.py:115
  159.4 76.3 %collective-permute-start.1 = (bf16[512,1024]{1,0:T(8,128)(2,1)}, bf16[512,1024]{1,0:T(8,128)(2,1)}, u32[]{:S(2)}, u32[]{:S(2)}) collective-permute-start(bf16[512,1024]{1,0:T(8,128)(2,1)} %all-gather.13.cloned.1.call-done), channel_id=1, source_target_pairs={{0,8},{8,0},{16,24},{24,16},{1,9},{9,1},{17,25},{25,17},{2,10},{10... | collective-permute-start | bytes 3145736 | tf_op jit(solution)/shard_map/ppermute | solution.py:17
  163.3 72.4 %copy-start.9 = (bf16[512,1024]{1,0:T(8,128)(2,1)S(1)}, bf16[512,1024]{1,0:T(8,128)(2,1)}, u32[]{:S(2)}) copy-start(bf16[512,1024]{1,0:T(8,128)(2,1)} %all-gather.13.cloned.1.call-done) | copy-start | bytes 3145732
  235.7 3.9 copy-start.2
  238.2 1.4 copy-start.4
  347.0 142.3 %reduce-scatter.6.cloned.1.call-start = ((), (), s32[]{:S(2)}) async-start(), calls=%async_computation.11 | async-start | bytes 5242880 | tf_op jit(solution)/shard_map/reduce_scatter | solution.py:117
  412.3 80.1 %copy-start.23 = (s32[15]{0:T(128)S(1)}, s32[15]{0:T(128)}, u32[]{:S(2)}) copy-start(s32[15]{0:T(128)} %param.9) | copy-start | bytes 184
  412.3 314.4 %all-gather.19.cloned.1.call-start = ((), (), s32[]{:S(2)}) async-start(), calls=%async_computation.12 | async-start | bytes 3145728 | tf_op jit(solution)/shard_map/all_gather | solution.py:125
  492.3 386.1 %all-gather.21.cloned.1.call-start = ((), (), s32[]{:S(2)}) async-start(), calls=%async_computation.13 | async-start | bytes 20971520 | tf_op jit(solution)/shard_map/all_gather | solution.py:158
  492.6 0.5 copy-start.21
  493.2 0.6 copy-start.13
  509.5 6.4 copy-start.19
  509.5 207.6 %all-to-all-start.1 = ((bf16[2,512,2048]{1,0,2:T(2,128)(2,1)}), bf16[2,512,2048]{1,0,2:T(2,128)(2,1)}, u32[]{:S(2)}, u32[]{:S(2)}) async-start(bf16[2,512,2048]{1,0,2:T(2,128)(2,1)} %copy.62), calls=%async_computation.3 | async-start | bytes 8388608 | tf_op jit(solution)/shard_map/all_to_all | solution.py:126
  514.5 548.2 %all-gather.23.cloned.1.call-start = ((), (), s32[]{:S(2)}) async-start(), calls=%async_computation.14 | async-start | bytes 18874368 | tf_op jit(solution)/shard_map/all_gather | solution.py:174
  514.6 0.7 copy-start.17
  516.0 0.6 copy-start.11
  516.7 2.9 copy-start.1
  516.8 3.5 copy-start.3
  516.8 4.1 copy-start.5
  726.7 6.4 slice-start
  726.7 6.4 slice-start.1
  911.4 0.7 copy-start.12
  911.4 0.7 copy-start.20
  911.4 0.8 copy-start.16
  911.4 0.9 copy-start.15
  911.5 316.0 %reduce-scatter.8.cloned.1.call-start = ((), (), s32[]{:S(2)}) async-start(), calls=%async_computation.15 | async-start | bytes 10485760 | tf_op jit(solution)/shard_map/reduce_scatter | solution.py:178
  1082.6 0.7 copy-start.18
  1082.6 0.7 copy-start.22
  1082.7 3.0 copy-start.6
  1082.7 144.8 %copy-start.7 = (bf16[2,1024,512]{2,1,0:T(8,128)(2,1)S(1)}, bf16[2,1024,512]{2,1,0:T(8,128)(2,1)}, u32[]{:S(2)}) copy-start(bf16[2,1024,512]{2,1,0:T(8,128)(2,1)} %param.17) | copy-start | bytes 6291460
  1082.7 144.8 %copy-start.14 = (pred[2,1024]{1,0:T(4,128)(4,1)S(1)}, pred[2,1024]{1,0:T(4,128)(4,1)}, u32[]{:S(2)}) copy-start(pred[2,1024]{1,0:T(4,128)(4,1)} %copy-done.13) | copy-start | bytes 6148
Sparse Core Ops, SparseCore 0:
  11.6 48.3 all-gather.8
  63.8 20.0 all-gather.10
  92.7 43.6 reduce-scatter.3
  138.9 20.4 all-gather.12
  160.8 171.4 all-gather.14
  347.1 55.7 all-gather.16
  412.4 76.7 reduce-scatter.5
  492.5 33.6 all-gather.18
  527.7 350.6 all-gather.20
  911.6 151.0 all-gather.22
  1082.8 144.6 reduce-scatter.7
